TPU v7x, 32 devices: a whole 2x2x4 slice. The times are simulated.
32 devices in a mesh: groups: 2 (over x), blk: 16 (over z, y, core).
Axes of the slice: x: 2, y: 2, z: 4, core: 2. Of those that a mesh axis runs over, the one named last changes fastest.
Arguments:
- query_inputs: bfloat16 [8192, 4096], P(('groups', 'blk')), parts along dimension 0, may hold values from -6 to 6
- query_grads: bfloat16 [8192, 4096], P(('groups', 'blk')), parts along dimension 0, may hold values from -6 to 6
- proj_in: bfloat16 [4096, 64], replicated, may hold values from -0.09375 to 0.09375
- proj_out: bfloat16 [4096, 64], replicated, may hold values from -0.09375 to 0.09375
- train_rows: bfloat16 [8192, 4096], P(('groups', 'blk')), parts along dimension 0, may hold values from -0.09375 to 0.09375
- token_owner: int32 [8192, 1], P(('groups', 'blk')), parts along dimension 0, may hold values from 0 to 15; in each aligned block of 256 rows (0 to 255, 256 to 511, ...) at most 64 rows name the same one
- token_slot: int32 [8192], P(('groups', 'blk')), parts along dimension 0, may hold values from 0 to 31
Outputs:
- influence: bfloat16 [12, 32, 8192], P(None, None, ('groups', 'blk')), parts along dimension 2
There are 2 independent parts, one for each index of `groups`. A program takes and returns all parts, laid end to end along the dimension named above; an argument that names none is the same for every part. Nothing has to cross between parts.
Inputs may be any that keep to these rules, and one draw needn't show every extreme that they name: `token_owner`: within the tokens of one device no owner is named by more than 64 tokens, a bound that some block reaches.
All inputs are finite; a program needn't handle non-finite values. Where the computation divides by a largest or mean magnitude, that divisor is 1e-20 or more.
Results may differ from a plain program's by a relative error of at most 0.0069.
Values may be sent and summed in bfloat16 or wider, within the bound.
A program may use at most 64 MiB of HBM per device.

v0:
```python
import functools

import jax
import jax.numpy as jnp
from jax import lax
from jax.experimental import pallas as pl
from jax.experimental.pallas import tpu as pltpu
from jax.sharding import PartitionSpec as P

DOC_DEV = 32
STOPS = 12
NEWTON_STEPS = 6
LEAD = 5
LANES = 128
DOC_GROUP = 8
GROUPS = DOC_DEV // DOC_GROUP
MESH = pl.DeviceIdType.MESH
VMEM_SPEC = pl.BlockSpec(memory_space=pltpu.VMEM)
F32 = jnp.float32
BF16 = jnp.bfloat16
CONTRACT_LAST = (((1,), (1,)), ((), ()))


def matmul(left, right):
    return jnp.dot(left, right, preferred_element_type=F32)


def halves(value):
    high = value.astype(BF16)
    return high, (value - high.astype(F32)).astype(BF16)


def left_parts(value, right_half):
    width = value.shape[1] // 2
    high = value.astype(BF16).astype(F32)
    low = value - high
    if right_half:
        high = pltpu.roll(high, width, 1)
    else:
        low = pltpu.roll(low, width, 1)
    is_left = lax.broadcasted_iota(jnp.int32, value.shape, 1) < width
    parts = jnp.where(is_left, high, low).astype(BF16)
    return jnp.concatenate([parts, parts], axis=1)


def pair_product(lefts, rights, right_half):
    high, low = zip(*[halves(value) for value in rights])
    high, low = jnp.concatenate(high, axis=1), jnp.concatenate(low, axis=1)
    product = matmul(
        jnp.concatenate([left_parts(value, right_half) for value in lefts], axis=0),
        jnp.concatenate([high, high, low, low], axis=0),
    )
    rows, cols = lefts[0].shape
    return product[:rows, :cols], product[rows:, cols:]


def dispatch_kernel(owners, capacity, far_in, far_grad, p_in, p_out, owner_row, slot_row,
                    recv_rows, recv_slot, x_in, x_grad, fetched, low, send_rows, send_slot,
                    rows_sent, rows_here, slot_sent, slot_here):
    me = lax.axis_index("blk")
    fetch_grad = pltpu.make_async_copy(far_grad, x_grad, fetched.at[0])
    fetch_in = pltpu.make_async_copy(far_in, x_in, fetched.at[1])
    fetch_grad.start()
    fetch_in.start()
    barrier = pltpu.get_barrier_semaphore()

    @pl.loop(1, owners)
    def _(ahead):
        pl.semaphore_signal(
            barrier, inc=1, device_id={"blk": lax.rem(me + ahead, owners)}, device_id_type=MESH
        )

    count = x_in.shape[0]
    width = p_in.shape[0]
    token = lax.broadcasted_iota(jnp.int32, (count, count), 0)
    other = lax.broadcasted_iota(jnp.int32, (count, count), 1)
    earlier = jnp.where(token < other, 1.0, 0.0).astype(BF16)
    owner_id = lax.broadcasted_iota(jnp.int32, (owners, count), 0)
    owner_hot = jnp.where(owner_id == owner_row[...], 1.0, 0.0)
    before = matmul(owner_hot.astype(BF16), earlier)
    rank = jnp.sum(before * owner_hot, axis=0, keepdims=True).astype(jnp.int32)
    position = owner_row[...] * capacity + rank
    place = lax.broadcasted_iota(jnp.int32, (owners * capacity, count), 0)
    placed = jnp.where(place == position, 1.0, 0.0).astype(BF16)
    for at, values, weights, fetch in (
        (0, x_grad, p_out, fetch_grad), (width, x_in, p_in, fetch_in)
    ):
        fetch.wait()
        low[:, at:at + width] = lax.dot_general(
            values[...], weights[...], CONTRACT_LAST, preferred_element_type=F32
        ).astype(BF16)
    send_rows[...] = matmul(placed, low[...]).astype(BF16).reshape(send_rows.shape)
    coded = jnp.where(owner_id == owner_row[...], slot_row[...] + 1, 0).astype(F32).astype(BF16)
    lane = lax.broadcasted_iota(jnp.int32, (LANES, count), 0)
    shift = lax.rem(me, LANES // capacity) * capacity
    spread = jnp.where(lane == rank + shift, 1.0, 0.0).astype(BF16)
    codes = lax.dot_general(coded, spread, CONTRACT_LAST, preferred_element_type=F32)
    codes = codes.astype(jnp.int32)
    for owner in range(owners):
        send_slot[owner] = codes[owner:owner + 1]
    pl.semaphore_wait(barrier, owners - 1)

    def copies(target, source, sem):
        to = {"blk": target}
        return (
            pltpu.make_async_remote_copy(
                src_ref=send_rows.at[target], dst_ref=recv_rows.at[source],
                send_sem=rows_sent.at[target], recv_sem=rows_here.at[sem],
                device_id=to, device_id_type=MESH),
            pltpu.make_async_remote_copy(
                src_ref=send_slot.at[target], dst_ref=recv_slot.at[source],
                send_sem=slot_sent.at[target], recv_sem=slot_here.at[sem],
                device_id=to, device_id_type=MESH),
        )

    @pl.loop(1, owners)
    def _(ahead):
        for copy in copies(lax.rem(me + ahead, owners), me, me):
            copy.start()

    recv_rows[me] = send_rows[me]
    recv_slot[me] = send_slot[me]

    @pl.loop(1, owners)
    def _(ahead):
        source = lax.rem(me + ahead, owners)
        for copy in copies(source, source, source):
            copy.wait_recv()

    @pl.loop(1, owners)
    def _(ahead):
        for copy in copies(lax.rem(me + ahead, owners), me, me):
            copy.wait_send()


def dispatch(x_in, x_grad, p_in, p_out, owner_row, slot_row):
    owners = lax.axis_size("blk")
    count, width = x_in.shape[0], p_in.shape[0]
    capacity = 4 * count // owners
    rows = (owners, capacity, 2 * width)
    slots = (owners, 1, LANES)
    return pl.pallas_call(
        functools.partial(dispatch_kernel, owners, capacity),
        out_shape=(jax.ShapeDtypeStruct(rows, BF16), jax.ShapeDtypeStruct(slots, jnp.int32)),
        in_specs=[pl.BlockSpec(memory_space=pl.ANY)] * 2 + [VMEM_SPEC] * 4,
        out_specs=(VMEM_SPEC, VMEM_SPEC),
        scratch_shapes=[
            pltpu.VMEM(x_in.shape, BF16),
            pltpu.VMEM(x_in.shape, BF16),
            pltpu.SemaphoreType.DMA((2,)),
            pltpu.VMEM((count, 2 * width), BF16),
            pltpu.VMEM(rows, BF16),
            pltpu.VMEM(slots, jnp.int32),
        ] + [pltpu.SemaphoreType.DMA((owners,))] * 4,
        compiler_params=pltpu.CompilerParams(collective_id=0, has_side_effects=True),
        name="dispatch",
    )(x_in, x_grad, p_in, p_out, owner_row, slot_row)


def prepare(recv_rows, recv_slot, turned, codes):
    owners, capacity, full = recv_rows.shape
    total = owners * capacity
    group = LANES // capacity
    rows = recv_rows[...].reshape(total, full)
    for part in range(total // LANES):
        span = slice(part * LANES, (part + 1) * LANES)
        turned[:, span] = rows[span].T
        code = recv_slot[part * group]
        for source in range(part * group + 1, (part + 1) * group):
            code = code + recv_slot[source]
        codes[:, span] = code


def query_group(step, recv_rows, turned, codes, flat, out):
    owners, capacity, full = recv_rows.shape
    width = full // 2
    row = lax.broadcasted_iota(jnp.int32, (width, full), 0)
    col = lax.broadcasted_iota(jnp.int32, (width, full), 1)
    left = col < width
    left_eye = jnp.where(row == col, 1.0, 0.0)
    right_eye = jnp.where(row + width == col, 1.0, 0.0)
    docs = range(DOC_GROUP)
    code = codes[...]
    counts, masked = [], []
    for doc in docs:
        hot = jnp.where(code == step * DOC_GROUP + doc + 1, 1.0, 0.0)
        counts.append(jnp.sum(hot, axis=1, keepdims=True))
        masked.append(turned[...] * hot.astype(BF16))
    rows = recv_rows[...].reshape(owners * capacity, full)
    half = DOC_GROUP // 2
    grams = [
        matmul(jnp.concatenate(masked[at:at + half], axis=0), rows) for at in (0, half)
    ]
    crossed, states = [], []
    for doc in docs:
        gram = grams[doc // half][doc % half * full:(doc % half + 1) * full]
        top, bottom = gram[:width], gram[width:]
        crossed.append(top)
        pair = []
        for outer in (top, pltpu.roll(bottom, width, 1)):
            damped = jnp.where(left, outer / (counts[doc] + 1.0), 0.0) + left_eye
            sums = jnp.sum(jnp.abs(damped), axis=1, keepdims=True)
            scale = 1.0 / jnp.max(sums, axis=0, keepdims=True)
            pair.append(left_eye - damped * scale + right_eye * scale)
        states.append(pair)
    for level in range(NEWTON_STEPS):
        for doc in docs:
            products = pair_product(states[doc], states[doc], False)
            states[doc] = [
                product + jnp.where(left, 0.0, state)
                for product, state in zip(products, states[doc])
            ]
    for doc in range(0, DOC_GROUP, 2):
        pair = (doc, doc + 1)
        tilted = pair_product(
            [states[d][0] for d in pair], [crossed[d] for d in pair], True)
        tilted = pair_product(tilted, [states[d][1] for d in pair], True)
        for d, value in zip(pair, tilted):
            flat[d * width:(d + 1) * width, :] = value

    near = lax.broadcasted_iota(jnp.int32, (DOC_GROUP, full), 1) < width
    for pair in range(width // 2):
        even = flat[pl.ds(2 * pair, DOC_GROUP, stride=width), :]
        odd = flat[pl.ds(2 * pair + 1, DOC_GROUP, stride=width), :]
        both = jnp.where(near, pltpu.roll(even, width, 1), odd)
        out[:, pair * full:(pair + 1) * full] = both.astype(BF16)


def query_scratch(recv_rows):
    owners, capacity, full = recv_rows.shape
    total = owners * capacity
    return [
        pltpu.VMEM((full, total), BF16),
        pltpu.VMEM((1, total), jnp.int32),
        pltpu.VMEM((DOC_GROUP * (full // 2), full), F32),
    ]


def queries_kernel(recv_rows, recv_slot, out, turned, codes, flat):
    prepare(recv_rows, recv_slot, turned, codes)

    @pl.loop(0, GROUPS)
    def _(step):
        query_group(step, recv_rows, turned, codes, flat, out.at[step])


def make_queries(recv_rows, recv_slot):
    width = recv_rows.shape[2] // 2
    return pl.pallas_call(
        queries_kernel,
        out_shape=jax.ShapeDtypeStruct((GROUPS, DOC_GROUP, width * width), BF16),
        in_specs=[VMEM_SPEC] * 2,
        out_specs=VMEM_SPEC,
        scratch_shapes=query_scratch(recv_rows),
        name="queries",
    )(recv_rows, recv_slot).reshape(DOC_DEV, width * width)


def score_into(out, index, block, train):
    out[index] = lax.dot_general(
        block[...], train[...], CONTRACT_LAST, preferred_element_type=F32
    ).astype(BF16)


def window_kernel(owners, queries, train, out, held, sent, here):
    me = lax.axis_index("blk")
    barrier = pltpu.get_barrier_semaphore()

    def peer(stop):
        return lax.rem(me + stop - LEAD + owners, owners)

    def source(stop):
        return lax.rem(me - stop + LEAD + owners, owners)

    def copy(stop):
        return pltpu.make_async_remote_copy(
            src_ref=queries, dst_ref=held.at[stop], send_sem=sent.at[stop],
            recv_sem=here.at[stop], device_id={"blk": peer(stop)}, device_id_type=MESH)

    others = [stop for stop in range(STOPS) if stop != LEAD]
    for stop in others:
        pl.semaphore_signal(
            barrier, inc=1, device_id={"blk": source(stop)}, device_id_type=MESH
        )
    pl.semaphore_wait(barrier, len(others))
    for stop in others:
        copy(stop).start()
    score_into(out, LEAD, queries, train)
    for stop in others:
        copy(stop).wait_recv()
        score_into(out, stop, held.at[stop], train)
    for stop in others:
        copy(stop).wait_send()


def grid_kernel(owners, recv_rows, recv_slot, train_far, out, turned, codes, flat, train, fetched, held,
                up_sent, down_sent, side_sent, twin_sent, here):
    lines = owners // 4
    me = lax.axis_index("blk")
    core = lax.rem(me, 2)
    side = lax.rem(me // 2, 2)
    line = me // 4
    twin = me + 1 - 2 * core
    across = me + 2 - 4 * side
    to_twin, to_across = 1 - 2 * core, 2 - 4 * side
    above, below = me + 4, me - 4
    has_up, has_down = line + 1 < lines, line > 0

    barrier = pltpu.get_barrier_semaphore()

    def greet(device):
        pl.semaphore_signal(barrier, inc=1, device_id={"blk": device}, device_id_type=MESH)

    greet(twin)
    greet(across)
    pl.when(has_up)(lambda: greet(above))
    pl.when(has_down)(lambda: greet(below))
    fetch = pltpu.make_async_copy(train_far, train, fetched)
    fetch.start()
    prepare(recv_rows, recv_slot, turned, codes)

    def wrapped(stop):
        return stop % owners if isinstance(stop, int) else lax.rem(stop + 3 * owners, owners)

    def wanted(stop):
        return wrapped(stop) < STOPS

    def either(first, second):
        return True if first is True or second is True else first | second

    def both(first, second):
        if first is True or second is True:
            return second if first is True else first
        return first & second

    def when(wish, act):
        if wish is True:
            act()
        elif wish is not False:
            pl.when(wish)(act)

    def reached(distance, way):
        if distance == 0:
            return True
        return line >= distance if way == 0 else line < lines - distance

    def place(stage, way, column):
        distance = stage - column
        if distance < 0 or (distance == 0 and way == 1):
            return None
        stop = LEAD - 4 * distance * (2 * way - 1)
        if column:
            stop = stop - to_across
        real = reached(distance, way)
        hands = []
        if column == 0:
            if way == 0:
                hands.append((both(real, has_up), 0, above, stop + 4))
            if way == 1 or distance == 0:
                hands.append((both(real, has_down), 1, below, stop - 4))
            sideways = either(wanted(stop + to_across), wanted(stop + to_across + to_twin))
            if distance == 0:
                sideways = True
            hands.append((both(real, sideways), 2, across, stop + to_across))
        else:
            real = both(real, either(wanted(stop), wanted(stop + to_twin)))
        hands.append((both(real, wanted(stop + to_twin)), 3, twin, stop + to_twin))
        twin_stop = stop - to_twin
        from_twin = both(reached(distance, way), wanted(twin_stop))
        hands = [(wish, sem, device, wrapped(theirs)) for wish, sem, device, theirs in hands]
        return wrapped(stop), real, hands, wrapped(twin_stop), from_twin

    sems = (up_sent, down_sent, side_sent, twin_sent)
    stages = []
    for stage in range(lines + 1):
        found = [place(stage, way, column) for column in range(2) for way in range(2)]
        stages.append([item for item in found if item is not None])

    def copy(group, mine, sem, device, theirs):
        return pltpu.make_async_remote_copy(
            src_ref=held.at[group, mine], dst_ref=held.at[group, theirs],
            send_sem=sems[sem].at[group, mine], recv_sem=here.at[group, theirs],
            device_id={"blk": device}, device_id_type=MESH)

    def arrive(group, mine):
        copy(group, mine, 3, twin, mine).wait_recv()

    def hand_on(group, item):
        for wish, sem, device, theirs in item[2]:
            when(wish, lambda: copy(group, item[0], sem, device, theirs).start())

    @pl.loop(0, GROUPS + lines)
    def _(step):
        @pl.when(step < GROUPS)
        def _():
            query_group(step, recv_rows, turned, codes, flat, held.at[step, LEAD])

            @pl.when(step == 0)
            def _():
                pl.semaphore_wait(barrier, 2 + has_up.astype(jnp.int32) + has_down.astype(jnp.int32))

            hand_on(step, stages[0][0])

        for stage in range(lines, 0, -1):
            group = step - stage

            @pl.when((group >= 0) & (group < GROUPS))
            def _():
                for item in stages[stage]:
                    when(item[1], lambda: arrive(group, item[0]))
                    hand_on(group, item)

        @pl.when(step >= lines)
        def _():
            group = step - lines
            for items in stages:
                for _, _, _, twin_stop, from_twin in items:
                    when(from_twin, lambda: arrive(group, twin_stop))
            pl.when(group == 0)(fetch.wait)
            block = held[group, :STOPS].reshape(STOPS * DOC_GROUP, train.shape[1])
            tile = lax.dot_general(block, train[...], CONTRACT_LAST, preferred_element_type=F32)
            out[group] = tile.astype(BF16).reshape(STOPS, DOC_GROUP, train.shape[0])

    @pl.loop(0, GROUPS)
    def _(group):
        for items in stages:
            for item in items:
                for wish, sem, device, theirs in item[2]:
                    when(wish, lambda: copy(group, item[0], sem, device, theirs).wait_send())


def influence_of(recv_rows, recv_slot, train):
    owners = lax.axis_size("blk")
    params = pltpu.CompilerParams(collective_id=1, has_side_effects=True)
    if owners % 4 == 0 and owners < 2 * STOPS:
        tiles = pl.pallas_call(
            functools.partial(grid_kernel, owners),
            out_shape=jax.ShapeDtypeStruct((GROUPS, STOPS, DOC_GROUP, train.shape[0]), BF16),
            in_specs=[VMEM_SPEC, VMEM_SPEC, pl.BlockSpec(memory_space=pl.ANY)],
            out_specs=VMEM_SPEC,
            scratch_shapes=query_scratch(recv_rows)
            + [pltpu.VMEM(train.shape, BF16), pltpu.SemaphoreType.DMA]
            + [pltpu.VMEM((GROUPS, owners, DOC_GROUP, train.shape[1]), BF16)]
            + [pltpu.SemaphoreType.DMA((GROUPS, owners))] * 5,
            compiler_params=params,
            name="influence",
        )(recv_rows, recv_slot, train)
        return tiles.transpose(1, 0, 2, 3).reshape(STOPS, DOC_DEV, train.shape[0])
    queries = make_queries(recv_rows, recv_slot)
    return pl.pallas_call(
        functools.partial(window_kernel, owners),
        out_shape=jax.ShapeDtypeStruct((STOPS, DOC_DEV, train.shape[0]), BF16),
        in_specs=[VMEM_SPEC] * 2,
        out_specs=VMEM_SPEC,
        scratch_shapes=[pltpu.VMEM((STOPS,) + queries.shape, BF16)]
        + [pltpu.SemaphoreType.DMA((STOPS,))] * 2,
        compiler_params=params,
        name="influence",
    )(queries, train)


def local(query_inputs, query_grads, proj_in, proj_out, train_rows, token_owner, token_slot):
    recv_rows, recv_slot = dispatch(
        query_inputs, query_grads, proj_in.T, proj_out.T,
        token_owner.reshape(1, -1), token_slot.reshape(1, -1),
    )
    return influence_of(recv_rows, recv_slot, train_rows)


def solution(mesh):
    placed = (
        P(("groups", "blk"), None),
        P(("groups", "blk"), None),
        P(),
        P(),
        P(("groups", "blk"), None),
        P(("groups", "blk"), None),
        P(("groups", "blk")),
    )
    return jax.shard_map(
        local,
        mesh=mesh,
        in_specs=placed,
        out_specs=P(None, None, ("groups", "blk")),
        check_vma=False,
    )
```

profile of v0, /device:TPU:0, one launch (start us, length us, event | category | flops | bytes accessed | tf_op | source)
XLA Modules:
  0.0 57.1 jit_solution(1357141355935695905)
XLA Ops:
  0.0 16.4 %dispatch.1 = (bf16[16,64,128]{2,1,0:T(8,128)(2,1)}, s32[16,1,128]{2,1,0:T(1,128)}) custom-call(bf16[256,4096]{1,0:T(8,128)(2,1)} %far_in.1, bf16[256,4096]{1,0:T(8,128)(2,1)} %far_grad.1, bf16[64,4096]{1,0:T(8,128)(2,1)} %bitcast.9, bf16[64,4096]{1,0:T(8,128)(2,1)} %bitcast.10, s32[1,256]{1,0:T(1,128)} %bitcast.11, s32[1,256]{1,0:T(1,128)} %bitcast.12), custom_call_target="tpu_custom_call" | custom-call | tf_op jit(solution)/shard_map/dispatch/pallas_call | solution.py:142
  16.5 39.0 %influence.1 = bf16[4,12,8,256]{3,2,1,0:T(8,128)(2,1)} custom-call(bf16[16,64,128]{2,1,0:T(8,128)(2,1)} %get-tuple-element.7.recv_rows, s32[16,1,128]{2,1,0:T(1,128)} %get-tuple-element.8.recv_slot, bf16[256,4096]{1,0:T(8,128)(2,1)} %train_far.1), custom_call_target="tpu_custom_call" | custom-call | tf_op jit(solution)/shard_map/influence/pallas_call | solution.py:436
  55.5 1.6 %copy_bitcast_fusion = bf16[12,32,256]{2,1,0:T(8,128)(2,1)} fusion(bf16[4,12,8,256]{3,2,1,0:T(8,128)(2,1)} %influence.1), kind=kLoop, calls=%fused_computation | loop fusion | bytes 393216 | tf_op jit(solution)/shard_map/reshape | solution.py:448
where the time goes:
time: 58.1 us; the launch traced here: 57.1 us
  Pallas kernels  55.5 us (96%)
  local copies, waits for them, and re-layouts  1.62 us (3%)
    pallas_call x1, Pallas kernels, influence_of(): pl.pallas_call(functools.partial(grid_kernel, owners), out_shape=jax.Shap...  39 us
    pallas_call x1, Pallas kernels, dispatch(): pl.pallas_call(functools.partial(dispatch_kernel, owners, capacity), out_...  16.4 us
    reshape x1, local copies, waits for them, and re-layouts, influence_of(): return tiles.transpose(1, 0, 2, 3).reshape(STOPS, DOC_DEV, train.shape[0])  1.62 us

commit v1 on v0

--- a/solution.py
+++ b/solution.py
@@ -294,27 +294,21 @@
 
 
 def grid_kernel(owners, recv_rows, recv_slot, train_far, out, turned, codes, flat, train, fetched, held,
-                up_sent, down_sent, side_sent, twin_sent, here):
-    lines = owners // 4
+                sent, here):
+    line_size = 4
     me = lax.axis_index("blk")
     core = lax.rem(me, 2)
     side = lax.rem(me // 2, 2)
-    line = me // 4
-    twin = me + 1 - 2 * core
-    across = me + 2 - 4 * side
+    line = me // line_size
     to_twin, to_across = 1 - 2 * core, 2 - 4 * side
-    above, below = me + 4, me - 4
-    has_up, has_down = line + 1 < lines, line > 0
+    twin, across = me + to_twin, me + to_across
+    above = lax.rem(me + line_size, owners)
+    below = lax.rem(me + owners - line_size, owners)
+    beyond = lax.rem(me + 2 * line_size, owners)
 
     barrier = pltpu.get_barrier_semaphore()
-
-    def greet(device):
+    for device in (twin, across, above, below, beyond):
         pl.semaphore_signal(barrier, inc=1, device_id={"blk": device}, device_id_type=MESH)
-
-    greet(twin)
-    greet(across)
-    pl.when(has_up)(lambda: greet(above))
-    pl.when(has_down)(lambda: greet(below))
     fetch = pltpu.make_async_copy(train_far, train, fetched)
     fetch.start()
     prepare(recv_rows, recv_slot, turned, codes)
@@ -325,97 +319,98 @@
     def wanted(stop):
         return wrapped(stop) < STOPS
 
-    def either(first, second):
-        return True if first is True or second is True else first | second
-
-    def both(first, second):
-        if first is True or second is True:
-            return second if first is True else first
-        return first & second
-
     def when(wish, act):
         if wish is True:
             act()
-        elif wish is not False:
+        else:
             pl.when(wish)(act)
 
-    def reached(distance, way):
-        if distance == 0:
-            return True
-        return line >= distance if way == 0 else line < lines - distance
-
-    def place(stage, way, column):
-        distance = stage - column
-        if distance < 0 or (distance == 0 and way == 1):
-            return None
-        stop = LEAD - 4 * distance * (2 * way - 1)
-        if column:
-            stop = stop - to_across
-        real = reached(distance, way)
-        hands = []
-        if column == 0:
-            if way == 0:
-                hands.append((both(real, has_up), 0, above, stop + 4))
-            if way == 1 or distance == 0:
-                hands.append((both(real, has_down), 1, below, stop - 4))
-            sideways = either(wanted(stop + to_across), wanted(stop + to_across + to_twin))
-            if distance == 0:
-                sideways = True
-            hands.append((both(real, sideways), 2, across, stop + to_across))
-        else:
-            real = both(real, either(wanted(stop), wanted(stop + to_twin)))
-        hands.append((both(real, wanted(stop + to_twin)), 3, twin, stop + to_twin))
-        twin_stop = stop - to_twin
-        from_twin = both(reached(distance, way), wanted(twin_stop))
-        hands = [(wish, sem, device, wrapped(theirs)) for wish, sem, device, theirs in hands]
-        return wrapped(stop), real, hands, wrapped(twin_stop), from_twin
-
-    sems = (up_sent, down_sent, side_sent, twin_sent)
-    stages = []
-    for stage in range(lines + 1):
-        found = [place(stage, way, column) for column in range(2) for way in range(2)]
-        stages.append([item for item in found if item is not None])
-
-    def copy(group, mine, sem, device, theirs):
+    def skips(some_core):
+        return (side == 0) & (some_core == 1) & (line != 1)
+
+    left = side == 0
+    own, plus, minus = LEAD, LEAD - line_size, LEAD + line_size
+    beside, beside_plus, beside_minus = (LEAD - to_across + turn for turn in (0, -line_size, line_size))
+    cross = LEAD - to_across - 2 * line_size
+    has_plus = jnp.logical_not(skips(core))
+    gives_plus = jnp.logical_not((side == 1) & (core == 1) & (line != 1))
+    twin_plus = jnp.logical_not(skips(1 - core))
+    has_cross = left | (core == 0)
+    twin_cross = left | (core == 1)
+    turns = ((side == 1) & (core == 0)) | (left & ((line == 0) | (line == 3)))
+
+    stages = (
+        (
+            (own, None, ((True, above, 0), (True, below, 1), (True, across, 2), (True, twin, 3))),
+        ),
+        (
+            (plus, True, ((gives_plus, across, 4), (True, twin, 5))),
+            (minus, True, ((True, across, 6), (True, twin, 7))),
+            (beside, True, ((turns, beyond, 8), (wanted(beside + to_twin), twin, 9))),
+        ),
+        (
+            (beside_plus, has_plus, ((left & (line == 1), below, 10),
+                                     (has_plus & wanted(beside_plus + to_twin), twin, 11))),
+            (beside_minus, True, ((left & (line == 2), above, 12),
+                                  (wanted(beside_minus + to_twin), twin, 13))),
+        ),
+        (
+            (cross, has_cross, ((has_cross & wanted(cross + to_twin), twin, 14),)),
+        ),
+    )
+    from_twin = (
+        (own, True), (plus, True), (minus, True), (beside, True), (beside_plus, twin_plus),
+        (beside_minus, True), (cross, twin_cross),
+    )
+
+    def copy(group, mine, sem, device):
+        theirs = wrapped(mine + device - me)
         return pltpu.make_async_remote_copy(
-            src_ref=held.at[group, mine], dst_ref=held.at[group, theirs],
-            send_sem=sems[sem].at[group, mine], recv_sem=here.at[group, theirs],
+            src_ref=held.at[group, wrapped(mine)], dst_ref=held.at[group, theirs],
+            send_sem=sent.at[sem, group], recv_sem=here.at[group, theirs],
             device_id={"blk": device}, device_id_type=MESH)
 
     def arrive(group, mine):
-        copy(group, mine, 3, twin, mine).wait_recv()
-
-    def hand_on(group, item):
-        for wish, sem, device, theirs in item[2]:
-            when(wish, lambda: copy(group, item[0], sem, device, theirs).start())
-
-    @pl.loop(0, GROUPS + lines)
+        pltpu.make_async_remote_copy(
+            src_ref=held.at[group, wrapped(mine)], dst_ref=held.at[group, wrapped(mine)],
+            send_sem=sent.at[0, group], recv_sem=here.at[group, wrapped(mine)],
+            device_id={"blk": twin}, device_id_type=MESH).wait_recv()
+
+    def run(group, stage):
+        for mine, comes, hands in stages[stage]:
+            if comes is not None:
+                when(comes, lambda: arrive(group, mine))
+            for wish, device, sem in hands:
+                when(wish, lambda: copy(group, mine, sem, device).start())
+
+    last = len(stages)
+
+    @pl.loop(0, GROUPS + last)
     def _(step):
         @pl.when(step < GROUPS)
         def _():
-            query_group(step, recv_rows, turned, codes, flat, held.at[step, LEAD])
+            query_group(step, recv_rows, turned, codes, flat, held.at[step, own])
 
             @pl.when(step == 0)
             def _():
-                pl.semaphore_wait(barrier, 2 + has_up.astype(jnp.int32) + has_down.astype(jnp.int32))
-
-            hand_on(step, stages[0][0])
-
-        for stage in range(lines, 0, -1):
+                pl.semaphore_wait(barrier, 5)
+
+            run(step, 0)
+
+        for stage in range(1, last):
             group = step - stage
 
             @pl.when((group >= 0) & (group < GROUPS))
             def _():
-                for item in stages[stage]:
-                    when(item[1], lambda: arrive(group, item[0]))
-                    hand_on(group, item)
-
-        @pl.when(step >= lines)
+                run(group, stage)
+
+        @pl.when(step >= last)
         def _():
-            group = step - lines
-            for items in stages:
-                for _, _, _, twin_stop, from_twin in items:
-                    when(from_twin, lambda: arrive(group, twin_stop))
+            group = step - last
+            for mine, comes in from_twin:
+                slot = mine - to_twin
+                wish = wanted(slot) if comes is True else comes & wanted(slot)
+                when(wish, lambda: arrive(group, slot))
             pl.when(group == 0)(fetch.wait)
             block = held[group, :STOPS].reshape(STOPS * DOC_GROUP, train.shape[1])
             tile = lax.dot_general(block, train[...], CONTRACT_LAST, preferred_element_type=F32)
@@ -424,15 +419,15 @@
     @pl.loop(0, GROUPS)
     def _(group):
         for items in stages:
-            for item in items:
-                for wish, sem, device, theirs in item[2]:
-                    when(wish, lambda: copy(group, item[0], sem, device, theirs).wait_send())
+            for mine, _, hands in items:
+                for wish, device, sem in hands:
+                    when(wish, lambda: copy(group, mine, sem, device).wait_send())
 
 
 def influence_of(recv_rows, recv_slot, train):
     owners = lax.axis_size("blk")
     params = pltpu.CompilerParams(collective_id=1, has_side_effects=True)
-    if owners % 4 == 0 and owners < 2 * STOPS:
+    if owners == 16:
         tiles = pl.pallas_call(
             functools.partial(grid_kernel, owners),
             out_shape=jax.ShapeDtypeStruct((GROUPS, STOPS, DOC_GROUP, train.shape[0]), BF16),
@@ -441,7 +436,7 @@
             scratch_shapes=query_scratch(recv_rows)
             + [pltpu.VMEM(train.shape, BF16), pltpu.SemaphoreType.DMA]
             + [pltpu.VMEM((GROUPS, owners, DOC_GROUP, train.shape[1]), BF16)]
-            + [pltpu.SemaphoreType.DMA((GROUPS, owners))] * 5,
+            + [pltpu.SemaphoreType.DMA((15, GROUPS)), pltpu.SemaphoreType.DMA((GROUPS, owners))],
             compiler_params=params,
             name="influence",
         )(recv_rows, recv_slot, train)

time: 58.1 us -> 50.7 us (0.87); the launches traced: 57.1 us -> 50.5 us
  Pallas kernels: 55.5 us -> 48.9 us
    pallas_call x1, Pallas kernels: 39 us -> 32.4 us  [influence_of(): pl.pallas_call(functools.partial(grid_kernel, owners), out_shape=jax.Shap...]
where the time goes in v1:
time: 50.7 us; the launch traced here: 50.5 us
  Pallas kernels  48.9 us (96%)
  local copies, waits for them, and re-layouts  1.62 us (3%)
    pallas_call x1, Pallas kernels, influence_of(): pl.pallas_call(functools.partial(grid_kernel, owners), out_shape=jax.Shap...  32.4 us
    pallas_call x1, Pallas kernels, dispatch(): pl.pallas_call(functools.partial(dispatch_kernel, owners, capacity), out_...  16.4 us
    reshape x1, local copies, waits for them, and re-layouts, influence_of(): return tiles.transpose(1, 0, 2, 3).reshape(STOPS, DOC_DEV, train.shape[0])  1.62 us

profile of v1, /device:TPU:0, one launch (start us, length us, event | category | flops | bytes accessed | tf_op | source)
XLA Modules:
  0.0 50.5 jit_solution(9567076797206512638)
XLA Ops:
  0.0 16.4 %dispatch.1 = (bf16[16,64,128]{2,1,0:T(8,128)(2,1)}, s32[16,1,128]{2,1,0:T(1,128)}) custom-call(bf16[256,4096]{1,0:T(8,128)(2,1)} %far_in.1, bf16[256,4096]{1,0:T(8,128)(2,1)} %far_grad.1, bf16[64,4096]{1,0:T(8,128)(2,1)} %bitcast.9, bf16[64,4096]{1,0:T(8,128)(2,1)} %bitcast.10, s32[1,256]{1,0:T(1,128)} %bitcast.11, s32[1,256]{1,0:T(1,128)} %bitcast.12), custom_call_target="tpu_custom_call" | custom-call | tf_op jit(solution)/shard_map/dispatch/pallas_call | solution.py:142
  16.5 32.4 %influence.1 = bf16[4,12,8,256]{3,2,1,0:T(8,128)(2,1)} custom-call(bf16[16,64,128]{2,1,0:T(8,128)(2,1)} %get-tuple-element.7.recv_rows, s32[16,1,128]{2,1,0:T(1,128)} %get-tuple-element.8.recv_slot, bf16[256,4096]{1,0:T(8,128)(2,1)} %train_far.1), custom_call_target="tpu_custom_call" | custom-call | tf_op jit(solution)/shard_map/influence/pallas_call | solution.py:431
  48.9 1.6 %copy_bitcast_fusion = bf16[12,32,256]{2,1,0:T(8,128)(2,1)} fusion(bf16[4,12,8,256]{3,2,1,0:T(8,128)(2,1)} %influence.1), kind=kLoop, calls=%fused_computation | loop fusion | bytes 393216 | tf_op jit(solution)/shard_map/reshape | solution.py:443

commit v2 on v1

--- a/solution.py
+++ b/solution.py
@@ -16,6 +16,7 @@
 GROUPS = DOC_DEV // DOC_GROUP
 MESH = pl.DeviceIdType.MESH
 VMEM_SPEC = pl.BlockSpec(memory_space=pltpu.VMEM)
+FAR_SPEC = pl.BlockSpec(memory_space=pl.ANY)
 F32 = jnp.float32
 BF16 = jnp.bfloat16
 CONTRACT_LAST = (((1,), (1,)), ((), ()))
@@ -54,24 +55,8 @@
     return product[:rows, :cols], product[rows:, cols:]
 
 
-def dispatch_kernel(owners, capacity, far_in, far_grad, p_in, p_out, owner_row, slot_row,
-                    recv_rows, recv_slot, x_in, x_grad, fetched, low, send_rows, send_slot,
-                    rows_sent, rows_here, slot_sent, slot_here):
-    me = lax.axis_index("blk")
-    fetch_grad = pltpu.make_async_copy(far_grad, x_grad, fetched.at[0])
-    fetch_in = pltpu.make_async_copy(far_in, x_in, fetched.at[1])
-    fetch_grad.start()
-    fetch_in.start()
-    barrier = pltpu.get_barrier_semaphore()
-
-    @pl.loop(1, owners)
-    def _(ahead):
-        pl.semaphore_signal(
-            barrier, inc=1, device_id={"blk": lax.rem(me + ahead, owners)}, device_id_type=MESH
-        )
-
-    count = x_in.shape[0]
-    width = p_in.shape[0]
+def pack(owners, capacity, owner_row, slot_row, send_slot, me):
+    count = owner_row.shape[1]
     token = lax.broadcasted_iota(jnp.int32, (count, count), 0)
     other = lax.broadcasted_iota(jnp.int32, (count, count), 1)
     earlier = jnp.where(token < other, 1.0, 0.0).astype(BF16)
@@ -82,14 +67,6 @@
     position = owner_row[...] * capacity + rank
     place = lax.broadcasted_iota(jnp.int32, (owners * capacity, count), 0)
     placed = jnp.where(place == position, 1.0, 0.0).astype(BF16)
-    for at, values, weights, fetch in (
-        (0, x_grad, p_out, fetch_grad), (width, x_in, p_in, fetch_in)
-    ):
-        fetch.wait()
-        low[:, at:at + width] = lax.dot_general(
-            values[...], weights[...], CONTRACT_LAST, preferred_element_type=F32
-        ).astype(BF16)
-    send_rows[...] = matmul(placed, low[...]).astype(BF16).reshape(send_rows.shape)
     coded = jnp.where(owner_id == owner_row[...], slot_row[...] + 1, 0).astype(F32).astype(BF16)
     lane = lax.broadcasted_iota(jnp.int32, (LANES, count), 0)
     shift = lax.rem(me, LANES // capacity) * capacity
@@ -98,6 +75,23 @@
     codes = codes.astype(jnp.int32)
     for owner in range(owners):
         send_slot[owner] = codes[owner:owner + 1]
+    return placed
+
+
+def greet_all(owners, me):
+    barrier = pltpu.get_barrier_semaphore()
+
+    @pl.loop(1, owners)
+    def _(ahead):
+        pl.semaphore_signal(
+            barrier, inc=1, device_id={"blk": lax.rem(me + ahead, owners)}, device_id_type=MESH
+        )
+
+    return barrier
+
+
+def exchange(owners, me, barrier, send_rows, send_slot, recv_rows, recv_slot,
+             rows_sent, rows_here, slot_sent, slot_here):
     pl.semaphore_wait(barrier, owners - 1)
 
     def copies(target, source, sem):
@@ -127,34 +121,70 @@
         for copy in copies(source, source, source):
             copy.wait_recv()
 
-    @pl.loop(1, owners)
-    def _(ahead):
-        for copy in copies(lax.rem(me + ahead, owners), me, me):
-            copy.wait_send()
-
-
-def dispatch(x_in, x_grad, p_in, p_out, owner_row, slot_row):
-    owners = lax.axis_size("blk")
-    count, width = x_in.shape[0], p_in.shape[0]
-    capacity = 4 * count // owners
+    def drain():
+        @pl.loop(1, owners)
+        def _(ahead):
+            for copy in copies(lax.rem(me + ahead, owners), me, me):
+                copy.wait_send()
+
+    return drain
+
+
+def gather(owners, capacity, far, near, fetched, low, send_rows, send_slot, recv_rows, recv_slot,
+           rows_sent, rows_here, slot_sent, slot_here):
+    me = lax.axis_index("blk")
+    fetches = [pltpu.make_async_copy(*pair, fetched.at[i]) for i, pair in enumerate(zip(far, near))]
+    for fetch in fetches:
+        fetch.start()
+    barrier = greet_all(owners, me)
+    owner_row, slot_row, p_out, x_grad, p_in, x_in = near
+    width = p_in.shape[0]
+    for fetch in fetches[:2]:
+        fetch.wait()
+    placed = pack(owners, capacity, owner_row, slot_row, send_slot, me)
+    for at, values, weights, waits in (
+        (0, x_grad, p_out, fetches[2:4]), (width, x_in, p_in, fetches[4:6])
+    ):
+        for fetch in waits:
+            fetch.wait()
+        low[:, at:at + width] = lax.dot_general(
+            values[...], weights[...], CONTRACT_LAST, preferred_element_type=F32
+        ).astype(BF16)
+    send_rows[...] = matmul(placed, low[...]).astype(BF16).reshape(send_rows.shape)
+    return exchange(owners, me, barrier, send_rows, send_slot, recv_rows, recv_slot,
+                    rows_sent, rows_here, slot_sent, slot_here)
+
+
+def dispatch_kernel(owners, capacity, *refs):
+    far, (recv_rows, recv_slot), near, rest = refs[:6], refs[6:8], refs[8:14], refs[14:]
+    drain = gather(owners, capacity, far, near, *rest[:4], recv_rows, recv_slot, *rest[4:])
+    drain()
+
+
+def gather_scratch(owners, capacity, near):
+    count, width = near[3].shape[0], near[2].shape[0]
+    return [pltpu.VMEM(item.shape, item.dtype) for item in near] + [
+        pltpu.SemaphoreType.DMA((len(near),)),
+        pltpu.VMEM((count, 2 * width), BF16),
+        pltpu.VMEM((owners, capacity, 2 * width), BF16),
+        pltpu.VMEM((owners, 1, LANES), jnp.int32),
+    ]
+
+
+def dispatch(owners, capacity, inputs):
+    width = inputs[2].shape[0]
     rows = (owners, capacity, 2 * width)
     slots = (owners, 1, LANES)
     return pl.pallas_call(
         functools.partial(dispatch_kernel, owners, capacity),
         out_shape=(jax.ShapeDtypeStruct(rows, BF16), jax.ShapeDtypeStruct(slots, jnp.int32)),
-        in_specs=[pl.BlockSpec(memory_space=pl.ANY)] * 2 + [VMEM_SPEC] * 4,
+        in_specs=[FAR_SPEC] * len(inputs),
         out_specs=(VMEM_SPEC, VMEM_SPEC),
-        scratch_shapes=[
-            pltpu.VMEM(x_in.shape, BF16),
-            pltpu.VMEM(x_in.shape, BF16),
-            pltpu.SemaphoreType.DMA((2,)),
-            pltpu.VMEM((count, 2 * width), BF16),
-            pltpu.VMEM(rows, BF16),
-            pltpu.VMEM(slots, jnp.int32),
-        ] + [pltpu.SemaphoreType.DMA((owners,))] * 4,
+        scratch_shapes=gather_scratch(owners, capacity, inputs)
+        + [pltpu.SemaphoreType.DMA((owners,))] * 4,
         compiler_params=pltpu.CompilerParams(collective_id=0, has_side_effects=True),
         name="dispatch",
-    )(x_in, x_grad, p_in, p_out, owner_row, slot_row)
+    )(*inputs)
 
 
 def prepare(recv_rows, recv_slot, turned, codes):
@@ -293,8 +323,11 @@
         copy(stop).wait_send()
 
 
-def grid_kernel(owners, recv_rows, recv_slot, train_far, out, turned, codes, flat, train, fetched, held,
-                sent, here):
+def grid_kernel(owners, capacity, *refs):
+    far, train_far, out, near = refs[:6], refs[6], refs[7], refs[8:14]
+    got, low, send_rows, send_slot, recv_rows, recv_slot = refs[14:20]
+    rows_sent, rows_here, slot_sent, slot_here = refs[20:24]
+    turned, codes, flat, train, fetched, held, sent, here = refs[24:]
     line_size = 4
     me = lax.axis_index("blk")
     core = lax.rem(me, 2)
@@ -306,9 +339,8 @@
     below = lax.rem(me + owners - line_size, owners)
     beyond = lax.rem(me + 2 * line_size, owners)
 
-    barrier = pltpu.get_barrier_semaphore()
-    for device in (twin, across, above, below, beyond):
-        pl.semaphore_signal(barrier, inc=1, device_id={"blk": device}, device_id_type=MESH)
+    drain = gather(owners, capacity, far, near, got, low, send_rows, send_slot, recv_rows, recv_slot,
+                   rows_sent, rows_here, slot_sent, slot_here)
     fetch = pltpu.make_async_copy(train_far, train, fetched)
     fetch.start()
     prepare(recv_rows, recv_slot, turned, codes)
@@ -391,10 +423,6 @@
         def _():
             query_group(step, recv_rows, turned, codes, flat, held.at[step, own])
 
-            @pl.when(step == 0)
-            def _():
-                pl.semaphore_wait(barrier, 5)
-
             run(step, 0)
 
         for stage in range(1, last):
@@ -422,26 +450,31 @@
             for mine, _, hands in items:
                 for wish, device, sem in hands:
                     when(wish, lambda: copy(group, mine, sem, device).wait_send())
-
-
-def influence_of(recv_rows, recv_slot, train):
-    owners = lax.axis_size("blk")
-    params = pltpu.CompilerParams(collective_id=1, has_side_effects=True)
+    drain()
+
+
+def influence_of(owners, capacity, inputs, train):
+    width = inputs[2].shape[0]
     if owners == 16:
+        recv_rows = jax.ShapeDtypeStruct((owners, capacity, 2 * width), BF16)
         tiles = pl.pallas_call(
-            functools.partial(grid_kernel, owners),
+            functools.partial(grid_kernel, owners, capacity),
             out_shape=jax.ShapeDtypeStruct((GROUPS, STOPS, DOC_GROUP, train.shape[0]), BF16),
-            in_specs=[VMEM_SPEC, VMEM_SPEC, pl.BlockSpec(memory_space=pl.ANY)],
+            in_specs=[FAR_SPEC] * (len(inputs) + 1),
             out_specs=VMEM_SPEC,
-            scratch_shapes=query_scratch(recv_rows)
+            scratch_shapes=gather_scratch(owners, capacity, inputs)
+            + [pltpu.VMEM(recv_rows.shape, BF16), pltpu.VMEM((owners, 1, LANES), jnp.int32)]
+            + [pltpu.SemaphoreType.DMA((owners,))] * 4
+            + query_scratch(recv_rows)
             + [pltpu.VMEM(train.shape, BF16), pltpu.SemaphoreType.DMA]
             + [pltpu.VMEM((GROUPS, owners, DOC_GROUP, train.shape[1]), BF16)]
             + [pltpu.SemaphoreType.DMA((15, GROUPS)), pltpu.SemaphoreType.DMA((GROUPS, owners))],
-            compiler_params=params,
+            compiler_params=pltpu.CompilerParams(
+                collective_id=0, has_side_effects=True, vmem_limit_bytes=32 << 20),
             name="influence",
-        )(recv_rows, recv_slot, train)
+        )(*inputs, train)
         return tiles.transpose(1, 0, 2, 3).reshape(STOPS, DOC_DEV, train.shape[0])
-    queries = make_queries(recv_rows, recv_slot)
+    queries = make_queries(*dispatch(owners, capacity, inputs))
     return pl.pallas_call(
         functools.partial(window_kernel, owners),
         out_shape=jax.ShapeDtypeStruct((STOPS, DOC_DEV, train.shape[0]), BF16),
@@ -449,17 +482,19 @@
         out_specs=VMEM_SPEC,
         scratch_shapes=[pltpu.VMEM((STOPS,) + queries.shape, BF16)]
         + [pltpu.SemaphoreType.DMA((STOPS,))] * 2,
-        compiler_params=params,
+        compiler_params=pltpu.CompilerParams(collective_id=1, has_side_effects=True),
         name="influence",
     )(queries, train)
 
 
 def local(query_inputs, query_grads, proj_in, proj_out, train_rows, token_owner, token_slot):
-    recv_rows, recv_slot = dispatch(
-        query_inputs, query_grads, proj_in.T, proj_out.T,
+    owners = lax.axis_size("blk")
+    inputs = (
         token_owner.reshape(1, -1), token_slot.reshape(1, -1),
+        proj_out.T, query_grads, proj_in.T, query_inputs, train_rows,
     )
-    return influence_of(recv_rows, recv_slot, train_rows)
+    *inputs, train = [pltpu.with_memory_space_constraint(item, pltpu.HBM) for item in inputs]
+    return influence_of(owners, 4 * query_inputs.shape[0] // owners, inputs, train)
 
 
 def solution(mesh):

time: 50.7 us -> 46.4 us (0.915)
  Pallas kernels: 48.9 us -> 45.5 us
  local copies, waits for them, and re-layouts: 1.62 us -> 0.7 us
    pallas_call x2 -> x1, Pallas kernels: 48.9 us -> 45.5 us  [influence_of(): pl.pallas_call(functools.partial(grid_kernel, owners, capacity), out_shap...]
    reshape x1, local copies, waits for them, and re-layouts: 1.62 us -> 0.7 us  [influence_of(): return tiles.transpose(1, 0, 2, 3).reshape(STOPS, DOC_DEV, train.shape[0])]
where the time goes in v2:
time: 46.4 us; the launch traced here: 46.2 us
  Pallas kernels  45.5 us (98%)
  local copies, waits for them, and re-layouts  0.7 us (2%)
    pallas_call x1, Pallas kernels, influence_of(): pl.pallas_call(functools.partial(grid_kernel, owners, capacity), out_shap...  45.5 us

profile of v2, /device:TPU:0, one launch (start us, length us, event | category | flops | bytes accessed | tf_op | source)
XLA Modules:
  0.0 46.2 jit_solution(12186208165296947471)
XLA Ops:
  0.0 45.5 %influence.1 = bf16[4,12,8,256]{3,2,1,0:T(8,128)(2,1)S(1)} custom-call(s32[1,256]{1,0:T(1,128)} %bitcast.11, s32[1,256]{1,0:T(1,128)} %bitcast.12, bf16[64,4096]{1,0:T(8,128)(2,1)} %bitcast.9, bf16[256,4096]{1,0:T(8,128)(2,1)} %refs_3_.1, bf16[64,4096]{1,0:T(8,128)(2,1)} %bitcast.10, bf16[256,4096]{1,0:T(8,128)(2,1)} %refs_5_.1, bf16[256,4096]{1,0:T(8,128)(2,1)} %refs_6_.1), custom_call_target="tpu_custom_call" | custom-call | tf_op jit(solution)/shard_map/influence/pallas_call | solution.py:460
  45.5 0.7 %copy_bitcast_fusion = bf16[12,32,256]{2,1,0:T(8,128)(2,1)} fusion(bf16[4,12,8,256]{3,2,1,0:T(8,128)(2,1)S(1)} %influence.1), kind=kLoop, calls=%fused_computation | loop fusion | bytes 393216 | tf_op jit(solution)/shard_map/reshape | solution.py:476

commit v3 on v2

--- a/solution.py
+++ b/solution.py
@@ -11,6 +11,8 @@
 STOPS = 12
 NEWTON_STEPS = 6
 LEAD = 5
+CUT = 2
+FLIP = 4
 LANES = 128
 DOC_GROUP = 8
 GROUPS = DOC_DEV // DOC_GROUP
@@ -29,30 +31,6 @@
 def halves(value):
     high = value.astype(BF16)
     return high, (value - high.astype(F32)).astype(BF16)
-
-
-def left_parts(value, right_half):
-    width = value.shape[1] // 2
-    high = value.astype(BF16).astype(F32)
-    low = value - high
-    if right_half:
-        high = pltpu.roll(high, width, 1)
-    else:
-        low = pltpu.roll(low, width, 1)
-    is_left = lax.broadcasted_iota(jnp.int32, value.shape, 1) < width
-    parts = jnp.where(is_left, high, low).astype(BF16)
-    return jnp.concatenate([parts, parts], axis=1)
-
-
-def pair_product(lefts, rights, right_half):
-    high, low = zip(*[halves(value) for value in rights])
-    high, low = jnp.concatenate(high, axis=1), jnp.concatenate(low, axis=1)
-    product = matmul(
-        jnp.concatenate([left_parts(value, right_half) for value in lefts], axis=0),
-        jnp.concatenate([high, high, low, low], axis=0),
-    )
-    rows, cols = lefts[0].shape
-    return product[:rows, :cols], product[rows:, cols:]
 
 
 def pack(owners, capacity, owner_row, slot_row, send_slot, me):
@@ -91,7 +69,7 @@
 
 
 def exchange(owners, me, barrier, send_rows, send_slot, recv_rows, recv_slot,
-             rows_sent, rows_here, slot_sent, slot_here):
+             rows_sent, rows_here, slot_sent, slot_here, during):
     pl.semaphore_wait(barrier, owners - 1)
 
     def copies(target, source, sem):
@@ -114,6 +92,8 @@
 
     recv_rows[me] = send_rows[me]
     recv_slot[me] = send_slot[me]
+    if during is not None:
+        during()
 
     @pl.loop(1, owners)
     def _(ahead):
@@ -131,7 +111,7 @@
 
 
 def gather(owners, capacity, far, near, fetched, low, send_rows, send_slot, recv_rows, recv_slot,
-           rows_sent, rows_here, slot_sent, slot_here):
+           rows_sent, rows_here, slot_sent, slot_here, during=None):
     me = lax.axis_index("blk")
     fetches = [pltpu.make_async_copy(*pair, fetched.at[i]) for i, pair in enumerate(zip(far, near))]
     for fetch in fetches:
@@ -152,7 +132,7 @@
         ).astype(BF16)
     send_rows[...] = matmul(placed, low[...]).astype(BF16).reshape(send_rows.shape)
     return exchange(owners, me, barrier, send_rows, send_slot, recv_rows, recv_slot,
-                    rows_sent, rows_here, slot_sent, slot_here)
+                    rows_sent, rows_here, slot_sent, slot_here, during)
 
 
 def dispatch_kernel(owners, capacity, *refs):
@@ -201,14 +181,34 @@
         codes[:, span] = code
 
 
+def beside_each_other(value, left):
+    high, low = halves(value)
+    right = (1.0 - left.astype(F32)).astype(BF16)
+    tops = jnp.concatenate([high * left, low * left], axis=1)
+    bottoms = jnp.concatenate([high * right, low * right], axis=1)
+    return jnp.concatenate([tops, bottoms, tops, bottoms], axis=0)
+
+
+def stack(values):
+    return jnp.concatenate([jnp.concatenate(halves(value), axis=1) for value in values], axis=0)
+
+
+def times(lefts, weights):
+    product = matmul(stack(lefts), weights)
+    lanes = product.shape[1] // 2
+    product = product[:, :lanes] + product[:, lanes:]
+    rows = lefts[0].shape[0]
+    return [product[at * rows:(at + 1) * rows] for at in range(len(lefts))]
+
+
 def query_group(step, recv_rows, turned, codes, flat, out):
     owners, capacity, full = recv_rows.shape
     width = full // 2
     row = lax.broadcasted_iota(jnp.int32, (width, full), 0)
     col = lax.broadcasted_iota(jnp.int32, (width, full), 1)
-    left = col < width
-    left_eye = jnp.where(row == col, 1.0, 0.0)
-    right_eye = jnp.where(row + width == col, 1.0, 0.0)
+    left = lax.broadcasted_iota(jnp.int32, (1, full), 1) < width
+    eye = jnp.where((row == col) | (row + width == col), 1.0, 0.0)
+    left_half = jnp.where(col < width, 1.0, 0.0).astype(BF16)
     docs = range(DOC_GROUP)
     code = codes[...]
     counts, masked = [], []
@@ -221,33 +221,33 @@
     grams = [
         matmul(jnp.concatenate(masked[at:at + half], axis=0), rows) for at in (0, half)
     ]
-    crossed, states = [], []
+    states, sums = [], []
     for doc in docs:
         gram = grams[doc // half][doc % half * full:(doc % half + 1) * full]
         top, bottom = gram[:width], gram[width:]
-        crossed.append(top)
-        pair = []
-        for outer in (top, pltpu.roll(bottom, width, 1)):
-            damped = jnp.where(left, outer / (counts[doc] + 1.0), 0.0) + left_eye
-            sums = jnp.sum(jnp.abs(damped), axis=1, keepdims=True)
-            scale = 1.0 / jnp.max(sums, axis=0, keepdims=True)
-            pair.append(left_eye - damped * scale + right_eye * scale)
-        states.append(pair)
+        damped = jnp.where(left, top, bottom) / (counts[doc] + 1.0) + eye
+        spread = jnp.sum(jnp.abs(damped), axis=0, keepdims=True)
+        bounds = [
+            jnp.max(jnp.where(side, spread, 0.0), axis=1, keepdims=True)
+            for side in (left, jnp.logical_not(left))
+        ]
+        scale = jnp.where(left, 1.0 / bounds[0], 1.0 / bounds[1])
+        states.append(eye - damped * scale)
+        sums.append(jnp.where(left, eye, top) * scale)
     for level in range(NEWTON_STEPS):
         for doc in docs:
-            products = pair_product(states[doc], states[doc], False)
-            states[doc] = [
-                product + jnp.where(left, 0.0, state)
-                for product, state in zip(products, states[doc])
-            ]
-    for doc in range(0, DOC_GROUP, 2):
-        pair = (doc, doc + 1)
-        tilted = pair_product(
-            [states[d][0] for d in pair], [crossed[d] for d in pair], True)
-        tilted = pair_product(tilted, [states[d][1] for d in pair], True)
-        for d, value in zip(pair, tilted):
-            flat[d * width:(d + 1) * width, :] = value
-
+            state, total = states[doc], sums[doc]
+            weights = beside_each_other(state, left_half)
+            if level < NEWTON_STEPS - 1:
+                states[doc], more = times([state, total], weights)
+            else:
+                more, = times([total], weights)
+            sums[doc] = total + more
+    zeros = jnp.zeros((width, 2 * full), BF16)
+    for doc in docs:
+        pieces = stack([sums[doc]])
+        flat[doc * width:(doc + 1) * width, :], = times(
+            [sums[doc]], jnp.concatenate([pieces, zeros, pieces, zeros], axis=0))
     near = lax.broadcasted_iota(jnp.int32, (DOC_GROUP, full), 1) < width
     for pair in range(width // 2):
         even = flat[pl.ds(2 * pair, DOC_GROUP, stride=width), :]
@@ -327,7 +327,7 @@
     far, train_far, out, near = refs[:6], refs[6], refs[7], refs[8:14]
     got, low, send_rows, send_slot, recv_rows, recv_slot = refs[14:20]
     rows_sent, rows_here, slot_sent, slot_here = refs[20:24]
-    turned, codes, flat, train, fetched, held, sent, here = refs[24:]
+    turned, codes, flat, train, train_turned, fetched, held, sent, here = refs[24:]
     line_size = 4
     me = lax.axis_index("blk")
     core = lax.rem(me, 2)
@@ -339,10 +339,20 @@
     below = lax.rem(me + owners - line_size, owners)
     beyond = lax.rem(me + 2 * line_size, owners)
 
+    fetch = pltpu.make_async_copy(train_far, train, fetched)
+
+    def flip():
+        fetch.start()
+        fetch.wait()
+
+        @pl.loop(0, train.shape[1] // (FLIP * LANES))
+        def _(step):
+            for part in range(FLIP):
+                at = pl.multiple_of((step * FLIP + part) * LANES, LANES)
+                train_turned[pl.ds(at, LANES), :] = train[:, pl.ds(at, LANES)].T
+
     drain = gather(owners, capacity, far, near, got, low, send_rows, send_slot, recv_rows, recv_slot,
-                   rows_sent, rows_here, slot_sent, slot_here)
-    fetch = pltpu.make_async_copy(train_far, train, fetched)
-    fetch.start()
+                   rows_sent, rows_here, slot_sent, slot_here, flip)
     prepare(recv_rows, recv_slot, turned, codes)
 
     def wrapped(stop):
@@ -369,27 +379,33 @@
     twin_plus = jnp.logical_not(skips(1 - core))
     has_cross = left | (core == 0)
     twin_cross = left | (core == 1)
-    turns = ((side == 1) & (core == 0)) | (left & ((line == 0) | (line == 3)))
-
-    stages = (
-        (
-            (own, None, ((True, above, 0), (True, below, 1), (True, across, 2), (True, twin, 3))),
-        ),
-        (
-            (plus, True, ((gives_plus, across, 4), (True, twin, 5))),
-            (minus, True, ((True, across, 6), (True, twin, 7))),
-            (beside, True, ((turns, beyond, 8), (wanted(beside + to_twin), twin, 9))),
-        ),
-        (
-            (beside_plus, has_plus, ((left & (line == 1), below, 10),
-                                     (has_plus & wanted(beside_plus + to_twin), twin, 11))),
-            (beside_minus, True, ((left & (line == 2), above, 12),
-                                  (wanted(beside_minus + to_twin), twin, 13))),
-        ),
-        (
-            (cross, has_cross, ((has_cross & wanted(cross + to_twin), twin, 14),)),
-        ),
-    )
+
+    def hands_of(group):
+        late = group >= CUT
+        turns = ((side == 1) & (core == 0)) | (left & ((line == 0) | (line == 3) | late))
+        chains = left & jnp.logical_not(late)
+        return (
+            (
+                (own, None, ((True, above, 0), (True, below, 1), (True, across, 2), (True, twin, 3))),
+            ),
+            (
+                (beside, True, ((turns, beyond, 8), (wanted(beside + to_twin), twin, 9))),
+            ),
+            (
+                (plus, True, ((gives_plus, across, 4), (True, twin, 5))),
+                (minus, True, ((True, across, 6), (True, twin, 7))),
+            ),
+            (
+                (beside_plus, has_plus, ((chains & (line == 1), below, 10),
+                                         (has_plus & wanted(beside_plus + to_twin), twin, 11))),
+                (beside_minus, True, ((chains & (line == 2), above, 12),
+                                      (wanted(beside_minus + to_twin), twin, 13))),
+            ),
+            (
+                (cross, has_cross, ((has_cross & wanted(cross + to_twin), twin, 14),)),
+            ),
+        )
+
     from_twin = (
         (own, True), (plus, True), (minus, True), (beside, True), (beside_plus, twin_plus),
         (beside_minus, True), (cross, twin_cross),
@@ -409,24 +425,30 @@
             device_id={"blk": twin}, device_id_type=MESH).wait_recv()
 
     def run(group, stage):
-        for mine, comes, hands in stages[stage]:
+        for mine, comes, hands in hands_of(jnp.int32(group))[stage]:
             if comes is not None:
                 when(comes, lambda: arrive(group, mine))
             for wish, device, sem in hands:
                 when(wish, lambda: copy(group, mine, sem, device).start())
 
-    last = len(stages)
+    def sent_by(group):
+        for items in hands_of(jnp.int32(group)):
+            for mine, _, hands in items:
+                for wish, device, sem in hands:
+                    when(wish, lambda: copy(group, mine, sem, device).wait_send())
+
+    last = 4
 
     @pl.loop(0, GROUPS + last)
     def _(step):
         @pl.when(step < GROUPS)
         def _():
             query_group(step, recv_rows, turned, codes, flat, held.at[step, own])
-
             run(step, 0)
-
-        for stage in range(1, last):
-            group = step - stage
+            pl.when(step == GROUPS - 1)(drain)
+
+        for stage, lag in ((1, 1), (2, 1), (3, 2), (4, 3)):
+            group = step - lag
 
             @pl.when((group >= 0) & (group < GROUPS))
             def _():
@@ -435,22 +457,16 @@
         @pl.when(step >= last)
         def _():
             group = step - last
+            pl.when(group > 0)(lambda: sent_by(group - 1))
             for mine, comes in from_twin:
                 slot = mine - to_twin
                 wish = wanted(slot) if comes is True else comes & wanted(slot)
                 when(wish, lambda: arrive(group, slot))
-            pl.when(group == 0)(fetch.wait)
             block = held[group, :STOPS].reshape(STOPS * DOC_GROUP, train.shape[1])
-            tile = lax.dot_general(block, train[...], CONTRACT_LAST, preferred_element_type=F32)
+            tile = matmul(block, train_turned[...])
             out[group] = tile.astype(BF16).reshape(STOPS, DOC_GROUP, train.shape[0])
 
-    @pl.loop(0, GROUPS)
-    def _(group):
-        for items in stages:
-            for mine, _, hands in items:
-                for wish, device, sem in hands:
-                    when(wish, lambda: copy(group, mine, sem, device).wait_send())
-    drain()
+    sent_by(GROUPS - 1)
 
 
 def influence_of(owners, capacity, inputs, train):
@@ -466,7 +482,8 @@
             + [pltpu.VMEM(recv_rows.shape, BF16), pltpu.VMEM((owners, 1, LANES), jnp.int32)]
             + [pltpu.SemaphoreType.DMA((owners,))] * 4
             + query_scratch(recv_rows)
-            + [pltpu.VMEM(train.shape, BF16), pltpu.SemaphoreType.DMA]
+            + [pltpu.VMEM(train.shape, BF16), pltpu.VMEM(train.shape[::-1], BF16)]
+            + [pltpu.SemaphoreType.DMA]
             + [pltpu.VMEM((GROUPS, owners, DOC_GROUP, train.shape[1]), BF16)]
             + [pltpu.SemaphoreType.DMA((15, GROUPS)), pltpu.SemaphoreType.DMA((GROUPS, owners))],
             compiler_params=pltpu.CompilerParams(

time: 46.4 us -> 43.8 us (0.944)
  Pallas kernels: 45.5 us -> 43 us
    pallas_call x1, Pallas kernels: 45.5 us -> 43 us  [influence_of(): pl.pallas_call(functools.partial(grid_kernel, owners, capacity), out_shap...]
where the time goes in v3:
time: 43.8 us; the launch traced here: 43.7 us
  Pallas kernels  43 us (98%)
  local copies, waits for them, and re-layouts  0.7 us (2%)
    pallas_call x1, Pallas kernels, influence_of(): pl.pallas_call(functools.partial(grid_kernel, owners, capacity), out_shap...  43 us

profile of v3, /device:TPU:0, one launch (start us, length us, event | category | flops | bytes accessed | tf_op | source)
XLA Modules:
  0.0 43.7 jit_solution(13922330110571696885)
XLA Ops:
  0.0 43.0 %influence.1 = bf16[4,12,8,256]{3,2,1,0:T(8,128)(2,1)S(1)} custom-call(s32[1,256]{1,0:T(1,128)} %bitcast.11, s32[1,256]{1,0:T(1,128)} %bitcast.12, bf16[64,4096]{1,0:T(8,128)(2,1)} %bitcast.9, bf16[256,4096]{1,0:T(8,128)(2,1)} %refs_3_.1, bf16[64,4096]{1,0:T(8,128)(2,1)} %bitcast.10, bf16[256,4096]{1,0:T(8,128)(2,1)} %refs_5_.1, bf16[256,4096]{1,0:T(8,128)(2,1)} %refs_6_.1), custom_call_target="tpu_custom_call" | custom-call | tf_op jit(solution)/shard_map/influence/pallas_call | solution.py:476
  43.0 0.7 %copy_bitcast_fusion = bf16[12,32,256]{2,1,0:T(8,128)(2,1)} fusion(bf16[4,12,8,256]{3,2,1,0:T(8,128)(2,1)S(1)} %influence.1), kind=kLoop, calls=%fused_computation | loop fusion | bytes 393216 | tf_op jit(solution)/shard_map/reshape | solution.py:493

commit v4 on v3

--- a/solution.py
+++ b/solution.py
@@ -437,36 +437,45 @@
                 for wish, device, sem in hands:
                     when(wish, lambda: copy(group, mine, sem, device).wait_send())
 
-    last = 4
-
-    @pl.loop(0, GROUPS + last)
+    def run_if(group, stage):
+        @pl.when(group >= 0)
+        def _():
+            run(group, stage)
+
+    def score(group):
+        for mine, comes in from_twin:
+            slot = mine - to_twin
+            wish = wanted(slot) if comes is True else comes & wanted(slot)
+            when(wish, lambda: arrive(group, slot))
+        block = held[group, :STOPS].reshape(STOPS * DOC_GROUP, train.shape[1])
+        tile = matmul(block, train_turned[...])
+        out[group] = tile.astype(BF16).reshape(STOPS, DOC_GROUP, train.shape[0])
+
+    @pl.loop(0, GROUPS)
     def _(step):
-        @pl.when(step < GROUPS)
-        def _():
-            query_group(step, recv_rows, turned, codes, flat, held.at[step, own])
-            run(step, 0)
-            pl.when(step == GROUPS - 1)(drain)
-
-        for stage, lag in ((1, 1), (2, 1), (3, 2), (4, 3)):
-            group = step - lag
-
-            @pl.when((group >= 0) & (group < GROUPS))
-            def _():
-                run(group, stage)
-
-        @pl.when(step >= last)
-        def _():
-            group = step - last
-            pl.when(group > 0)(lambda: sent_by(group - 1))
-            for mine, comes in from_twin:
-                slot = mine - to_twin
-                wish = wanted(slot) if comes is True else comes & wanted(slot)
-                when(wish, lambda: arrive(group, slot))
-            block = held[group, :STOPS].reshape(STOPS * DOC_GROUP, train.shape[1])
-            tile = matmul(block, train_turned[...])
-            out[group] = tile.astype(BF16).reshape(STOPS, DOC_GROUP, train.shape[0])
-
-    sent_by(GROUPS - 1)
+        query_group(step, recv_rows, turned, codes, flat, held.at[step, own])
+        run(step, 0)
+        run_if(step - 2, 2)
+        run_if(step - 2, 1)
+
+    drain()
+    run(2, 1)
+    run(2, 2)
+    run(0, 3)
+    run(0, 4)
+    run(3, 1)
+    run(1, 3)
+    score(0)
+    run(3, 2)
+    run(1, 4)
+    score(1)
+    run(2, 3)
+    run(2, 4)
+    run(3, 3)
+    score(2)
+    run(3, 4)
+    score(3)
+    pl.loop(0, GROUPS)(sent_by)
 
 
 def influence_of(owners, capacity, inputs, train):

time: 43.8 us -> 42.7 us (0.975)
  Pallas kernels: 43 us -> 41.8 us
    pallas_call x1, Pallas kernels: 43 us -> 41.8 us  [influence_of(): pl.pallas_call(functools.partial(grid_kernel, owners, capacity), out_shap...]
where the time goes in v4:
time: 42.7 us; the launch traced here: 42.5 us
  Pallas kernels  41.8 us (98%)
  local copies, waits for them, and re-layouts  0.7 us (2%)
    pallas_call x1, Pallas kernels, influence_of(): pl.pallas_call(functools.partial(grid_kernel, owners, capacity), out_shap...  41.8 us

profile of v4, /device:TPU:0, one launch (start us, length us, event | category | flops | bytes accessed | tf_op | source)
XLA Modules:
  0.0 42.5 jit_solution(18267325280109119029)
XLA Ops:
  0.0 41.8 %influence.1 = bf16[4,12,8,256]{3,2,1,0:T(8,128)(2,1)S(1)} custom-call(s32[1,256]{1,0:T(1,128)} %bitcast.11, s32[1,256]{1,0:T(1,128)} %bitcast.12, bf16[64,4096]{1,0:T(8,128)(2,1)} %bitcast.9, bf16[256,4096]{1,0:T(8,128)(2,1)} %refs_3_.1, bf16[64,4096]{1,0:T(8,128)(2,1)} %bitcast.10, bf16[256,4096]{1,0:T(8,128)(2,1)} %refs_5_.1, bf16[256,4096]{1,0:T(8,128)(2,1)} %refs_6_.1), custom_call_target="tpu_custom_call" | custom-call | tf_op jit(solution)/shard_map/influence/pallas_call | solution.py:485
  41.8 0.7 %copy_bitcast_fusion = bf16[12,32,256]{2,1,0:T(8,128)(2,1)} fusion(bf16[4,12,8,256]{3,2,1,0:T(8,128)(2,1)S(1)} %influence.1), kind=kLoop, calls=%fused_computation | loop fusion | bytes 393216 | tf_op jit(solution)/shard_map/reshape | solution.py:502

commit v5 on v4

--- a/solution.py
+++ b/solution.py
@@ -183,9 +183,8 @@
 
 def beside_each_other(value, left):
     high, low = halves(value)
-    right = (1.0 - left.astype(F32)).astype(BF16)
     tops = jnp.concatenate([high * left, low * left], axis=1)
-    bottoms = jnp.concatenate([high * right, low * right], axis=1)
+    bottoms = jnp.concatenate([high, low], axis=1) - tops
     return jnp.concatenate([tops, bottoms, tops, bottoms], axis=0)
 
 
@@ -225,7 +224,7 @@
     for doc in docs:
         gram = grams[doc // half][doc % half * full:(doc % half + 1) * full]
         top, bottom = gram[:width], gram[width:]
-        damped = jnp.where(left, top, bottom) / (counts[doc] + 1.0) + eye
+        damped = jnp.where(left, top, bottom) * (1.0 / (counts[doc] + 1.0)) + eye
         spread = jnp.sum(jnp.abs(damped), axis=0, keepdims=True)
         bounds = [
             jnp.max(jnp.where(side, spread, 0.0), axis=1, keepdims=True)
@@ -386,7 +385,7 @@
         chains = left & jnp.logical_not(late)
         return (
             (
-                (own, None, ((True, above, 0), (True, below, 1), (True, across, 2), (True, twin, 3))),
+                (own, None, ((True, across, 2), (True, above, 0), (True, below, 1), (True, twin, 3))),
             ),
             (
                 (beside, True, ((turns, beyond, 8), (wanted(beside + to_twin), twin, 9))),
@@ -459,17 +458,17 @@
         run_if(step - 2, 1)
 
     drain()
+    run(2, 2)
     run(2, 1)
-    run(2, 2)
     run(0, 3)
+    run(3, 1)
     run(0, 4)
-    run(3, 1)
+    score(0)
     run(1, 3)
-    score(0)
     run(3, 2)
     run(1, 4)
+    run(2, 3)
     score(1)
-    run(2, 3)
     run(2, 4)
     run(3, 3)
     score(2)

time: 42.7 us -> 42.5 us (level)
  no operation moved by 1% of the time
where the time goes in v5:
time: 42.5 us; the launch traced here: 42.2 us
  Pallas kernels  41.5 us (98%)
  local copies, waits for them, and re-layouts  0.7 us (2%)
    pallas_call x1, Pallas kernels, influence_of(): pl.pallas_call(functools.partial(grid_kernel, owners, capacity), out_shap...  41.5 us

profile of v5, /device:TPU:0, one launch (start us, length us, event | category | flops | bytes accessed | tf_op | source)
XLA Modules:
  0.0 42.2 jit_solution(6484742426106142195)
XLA Ops:
  0.0 41.5 %influence.1 = bf16[4,12,8,256]{3,2,1,0:T(8,128)(2,1)S(1)} custom-call(s32[1,256]{1,0:T(1,128)} %bitcast.11, s32[1,256]{1,0:T(1,128)} %bitcast.12, bf16[64,4096]{1,0:T(8,128)(2,1)} %bitcast.9, bf16[256,4096]{1,0:T(8,128)(2,1)} %refs_3_.1, bf16[64,4096]{1,0:T(8,128)(2,1)} %bitcast.10, bf16[256,4096]{1,0:T(8,128)(2,1)} %refs_5_.1, bf16[256,4096]{1,0:T(8,128)(2,1)} %refs_6_.1), custom_call_target="tpu_custom_call" | custom-call | tf_op jit(solution)/shard_map/influence/pallas_call | solution.py:484
  41.5 0.7 %copy_bitcast_fusion = bf16[12,32,256]{2,1,0:T(8,128)(2,1)} fusion(bf16[4,12,8,256]{3,2,1,0:T(8,128)(2,1)S(1)} %influence.1), kind=kLoop, calls=%fused_computation | loop fusion | bytes 393216 | tf_op jit(solution)/shard_map/reshape | solution.py:501
